TPU v7x, 128 devices: a whole 4x4x4 slice. The times are simulated.
128 devices in a mesh: req: 16 (over y, x), exp: 8 (over z, core).
Axes of the slice: x: 4, y: 4, z: 4, core: 2. Of those that a mesh axis runs over, the one named last changes fastest.
Arguments:
- attention_out: bfloat16 [2048, 4096], P('req'), may hold values from -6 to 6
- residual: bfloat16 [2048, 4096], P('req', 'exp'), may hold values from -6 to 6
- w_out: bfloat16 [4096, 4096], P('req', 'exp'), may hold values from -0.09375 to 0.09375
- router_w: float32 [4096, 8], P('exp'), may hold values from -0.09375 to 0.09375
- norm_gain: float32 [4096], P('exp'), may hold values from 0.5 to 1.5
- page_pool: bfloat16 [4096, 8, 2048], P('req', None, 'exp'), may hold values from -6 to 6
- page_table: int32 [2048, 2], P('req'), may hold values from 0 to 255, as said below
- cache_len: int32 [2048], P('req'), may hold values from 1 to 16
- came_from: int32 [2048], replicated, may hold values from 0 to 2047, as said below
- routes: int32 [2048, 2], P('req'), may hold values from 0 to 7, all different within a row; in each aligned block of 128 rows (0 to 127, 128 to 255, ...) at most 64 rows name the same one
- w_gate: bfloat16 [16, 4096, 7168], P('req', None, 'exp'), as said below
- w_up: bfloat16 [16, 4096, 7168], P('req', None, 'exp'), as said below
- w_down: bfloat16 [16, 7168, 4096], P('req', 'exp'), as said below
Outputs:
- mixed: float32 [2048, 4096], P('req', 'exp')
- new_pages: bfloat16 [2048, 2, 8, 2048], P('req', None, None, 'exp')
Inputs may be any that keep to these rules, and one draw needn't show every extreme that they name: page_table's entries for the requests of one req group are distinct. came_from is a permutation; from each req group 4 rows go to each of the other 15 groups, each group receives 4 rows from each of them, and all other rows keep their place. `routes`: within the rows of one req group every expert is named by at most 64 rows, and some expert by exactly 64 rows in some group. `w_gate`: slices e and e + 8 along the first dimension are equal. `w_up`: slices e and e + 8 along the first dimension are equal. `w_down`: slices e and e + 8 along the first dimension are equal.
All inputs are finite; a program needn't handle non-finite values.
Results may differ from a plain program's by a relative error of at most 0.0055.
Values may be sent and summed in bfloat16 or wider, within the bound.
A program may use at most 128 MiB of HBM per device.

v0:
```python
import jax
import jax.numpy as jnp
from jax import lax
from jax.sharding import PartitionSpec as P

D = 4096
CAP = 32
MIG_PAIR = 4
EPSILON = 1e-05


def pick_rows(source, row_index, live_slot):
    taken_rows = jnp.take(source, row_index, axis=0)
    return jnp.where(live_slot[:, None], taken_rows, jnp.zeros((), source.dtype))


def body(
    attention_out,
    residual,
    w_out,
    router_w,
    norm_gain,
    page_pool,
    page_table,
    cache_len,
    came_from,
    routes,
    w_gate,
    w_up,
    w_down,
):
    groups = lax.axis_size("req")
    own_group = lax.axis_index("req")
    row_req = attention_out.shape[0]
    rows_all = came_from.shape[0]
    pages_req = page_table.shape[1]
    page_len = page_pool.shape[1]
    kv_slice = page_pool.shape[2]
    experts = groups // 2
    targets = jnp.arange(groups, dtype=jnp.int32)
    local_ids = jnp.arange(row_req, dtype=jnp.int32)
    dest_of = (
        jnp.zeros((rows_all,), jnp.int32).at[came_from].set(jnp.arange(rows_all, dtype=jnp.int32))
    )
    dest_group = dest_of // row_req
    dest_hot = (
        (dest_group[:, None] == targets[None, :]).astype(jnp.int32).reshape(groups, row_req, groups)
    )
    pair_rank = jnp.sum((jnp.cumsum(dest_hot, axis=1) - dest_hot) * dest_hot, axis=2).reshape(
        rows_all
    )
    own_dest = lax.dynamic_slice_in_dim(dest_group, own_group * row_req, row_req)
    own_rank = lax.dynamic_slice_in_dim(pair_rank, own_group * row_req, row_req)
    chosen_send = (
        (own_dest[None, None, :] == targets[:, None, None])
        & (own_rank[None, None, :] == jnp.arange(MIG_PAIR, dtype=jnp.int32)[None, :, None])
        & (targets[:, None, None] != own_group)
    )
    send_index = jnp.sum(jnp.where(chosen_send, local_ids[None, None, :], 0), axis=2).reshape(-1)
    send_live = jnp.any(chosen_send, axis=2).reshape(-1)
    page_rows = jnp.take(page_pool, page_table.reshape(-1), axis=0).reshape(
        row_req, pages_req, page_len, kv_slice
    )
    position = (
        jnp.arange(pages_req, dtype=jnp.int32)[:, None] * page_len
        + jnp.arange(page_len, dtype=jnp.int32)[None, :]
    )
    kept_mask = position[None, :, :] < cache_len[:, None, None]
    page_rows = jnp.where(kept_mask[..., None], page_rows, jnp.zeros((), page_rows.dtype)).reshape(
        row_req, -1
    )
    moved_attn, moved_resid, moved_pages = (
        lax.all_to_all(
            pick_rows(attention_out, send_index, send_live),
            "req",
            split_axis=0,
            concat_axis=0,
            tiled=True,
        ),
        lax.all_to_all(
            pick_rows(residual, send_index, send_live),
            "req",
            split_axis=0,
            concat_axis=0,
            tiled=True,
        ),
        lax.all_to_all(
            pick_rows(page_rows, send_index, send_live),
            "req",
            split_axis=0,
            concat_axis=0,
            tiled=True,
        ),
    )
    new_source = lax.dynamic_slice_in_dim(came_from, own_group * row_req, row_req)
    source_group = new_source // row_req
    stays_home = source_group == own_group
    arrival = jnp.where(
        stays_home,
        new_source - own_group * row_req,
        row_req + source_group * MIG_PAIR + jnp.take(pair_rank, new_source),
    )
    attn_new = jnp.take(jnp.concatenate([attention_out, moved_attn], axis=0), arrival, axis=0)
    resid_new = jnp.take(jnp.concatenate([residual, moved_resid], axis=0), arrival, axis=0)
    new_pages = jnp.take(
        jnp.concatenate([page_rows, moved_pages], axis=0), arrival, axis=0
    ).reshape(row_req, pages_req, page_len, kv_slice)
    projected = jnp.dot(
        attn_new,
        lax.all_gather(w_out, "req", axis=0, tiled=True),
        preferred_element_type=jnp.float32,
    )
    hidden = resid_new.astype(jnp.float32) + projected
    squares = jnp.sum(hidden * hidden, axis=1)
    scaled = hidden * norm_gain[None, :]
    total_sq = lax.psum(squares, "exp")
    inverse = lax.rsqrt(total_sq / D + EPSILON)
    normed = scaled * inverse[:, None]
    logits = lax.psum(jnp.dot(normed, router_w, precision=lax.Precision.HIGHEST), "exp")
    normed_rows = normed.astype(jnp.bfloat16)
    expert_ids = jnp.arange(experts, dtype=jnp.int32)
    chosen = jnp.sum(
        jnp.where(routes[:, :, None] == expert_ids[None, None, :], logits[:, None, :], 0.0), axis=2
    )
    gate_first = jax.nn.sigmoid(chosen[:, 0] - chosen[:, 1])
    gate_second = jax.nn.sigmoid(chosen[:, 1] - chosen[:, 0])
    flat_routes = routes.reshape(-1)
    expert_hot = (flat_routes[:, None] == expert_ids[None, :]).astype(jnp.int32)
    expert_rank = jnp.sum((jnp.cumsum(expert_hot, axis=0) - expert_hot) * expert_hot, axis=1)
    target_dev = flat_routes + experts * (expert_rank % 2)
    slot_index = expert_rank // 2
    assign_ids = jnp.arange(flat_routes.shape[0], dtype=jnp.int32)
    chosen_slot = (target_dev[None, None, :] == targets[:, None, None]) & (
        slot_index[None, None, :] == jnp.arange(CAP, dtype=jnp.int32)[None, :, None]
    )
    slot_source = jnp.sum(
        jnp.where(chosen_slot, assign_ids[None, None, :] // 2, 0), axis=2
    ).reshape(-1)
    slot_live = jnp.any(chosen_slot, axis=2).reshape(-1)
    outgoing = pick_rows(normed_rows, slot_source, slot_live)
    arrived = lax.all_to_all(outgoing, "req", split_axis=0, concat_axis=0, tiled=True)
    rows_full = lax.all_gather(arrived, "exp", axis=1, tiled=True)
    gate_h = jnp.dot(rows_full, w_gate[0], preferred_element_type=jnp.float32)
    up_h = jnp.dot(rows_full, w_up[0], preferred_element_type=jnp.float32)
    active = (jax.nn.silu(gate_h) * up_h).astype(jnp.bfloat16)
    partial_value = lax.optimization_barrier(
        jnp.dot(active, w_down[0], preferred_element_type=jnp.float32).astype(jnp.bfloat16)
    )
    lookup = target_dev * CAP + slot_index
    returned = lax.all_to_all(partial_value, "req", split_axis=0, concat_axis=0, tiled=True)
    taken_rows = jnp.take(returned, lookup, axis=0).reshape(row_req, 2, -1)
    weighted = gate_first[:, None] * taken_rows[:, 0].astype(jnp.float32) + gate_second[
        :, None
    ] * taken_rows[:, 1].astype(jnp.float32)
    expert_part = lax.psum_scatter(
        weighted.astype(jnp.bfloat16), "exp", scatter_dimension=1, tiled=True
    ).astype(jnp.float32)
    mixed = hidden + expert_part
    return (mixed, new_pages)


def solution(mesh):
    in_specs = (
        P("req", None),
        P("req", "exp"),
        P("req", "exp"),
        P("exp", None),
        P("exp"),
        P("req", None, "exp"),
        P("req", None),
        P("req"),
        P(),
        P("req", None),
        P("req", None, "exp"),
        P("req", None, "exp"),
        P("req", "exp", None),
    )
    out_specs = (P("req", "exp"), P("req", None, None, "exp"))
    return jax.shard_map(body, mesh=mesh, in_specs=in_specs, out_specs=out_specs, check_vma=False)
```

profile of v0, /device:TPU:0, one launch (start us, length us, event | category | flops | bytes accessed | tf_op | source)
XLA Modules:
  0.0 285.6 jit_solution(12334850241228818001)
XLA Ops:
  8.6 8.0 %scatter_custom_fusion = s32[2048]{0:T(1024)S(1)} fusion(s32[2048]{0:T(1024)S(1)} %compare_select_fusion.1, s32[2048]{0:T(1024)S(1)} %iota.72, s32[]{:T(128)} %constant.182.clone.1), kind=kCustom, calls=%fused_computation.92 | custom fusion | bytes 8196 | tf_op jit(solution)/shard_map/scatter | solution.py:43
  16.9 2.8 select_reduce_fusion
  20.7 1.6 gather_fusion.1
  23.1 7.1 %all-to-all-start = ((bf16[16,4,512]{2,1,0:T(4,128)(2,1)}), bf16[16,4,512]{2,1,0:T(4,128)(2,1)S(1)}, u32[]{:S(2)}, u32[]{:S(2)}) async-start(bf16[16,4,512]{2,1,0:T(4,128)(2,1)} %select_select_fusion.4), calls=%async_computation | async-start | bytes 131072 | tf_op jit(solution)/shard_map/all_to_all | solution.py:80
  35.3 1.1 gather_fusion
  38.1 1.1 copy.133
  39.2 1.7 gather_fusion.5
  41.0 2.4 gather.47
  44.2 1.6 select_select_fusion
  49.6 7.2 %all-to-all-start.1 = ((bf16[16,4,4096]{2,1,0:T(4,128)(2,1)}), bf16[16,4,4096]{2,1,0:T(4,128)(2,1)S(1)}, u32[]{:S(2)}, u32[]{:S(2)}) async-start(bf16[16,4,4096]{2,1,0:T(4,128)(2,1)} %all_to_all.38), calls=%async_computation.1 | async-start | bytes 1048576 | tf_op jit(solution)/shard_map/all_to_all | solution.py:73
  58.2 13.6 %all-to-all-done.1 = bf16[16,4,4096]{2,1,0:T(4,128)(2,1)S(1)} async-done(((bf16[16,4,4096]{2,1,0:T(4,128)(2,1)}), bf16[16,4,4096]{2,1,0:T(4,128)(2,1)S(1)}, u32[]{:S(2)}, u32[]{:S(2)}) %all-to-all-start.1) | async-done | bytes 524320 | tf_op jit(solution)/shard_map/all_to_all | solution.py:73
  72.2 1.2 gather_fusion.7
  73.4 3.0 %multiply_reduce_fusion = (f32[128]{0:T(128)S(1)}, f32[128,512]{1,0:T(8,128)S(1)}) fusion(bf16[4096,512]{1,0:T(8,128)(2,1)} %all-gather.3.cloned.1.call-done, bf16[128,4096]{1,0:T(8,128)(2,1)S(1)} %gather_fusion.7, pred[128]{0:T(512)(128)(4,1)S(1)} %get-tuple-element.4, bf16[128,512]{1,0:T(8,128)(2,1)S(1)} %gather_fusion.2), kind=kOutput, calls=%fused_computation.47 | convolution fusion | flops 537722752 | bytes 5636736 | tf_op jit(solution)/shard_map/dot_general | solution.py:108
  76.4 14.3 %psum.14 = f32[128]{0:T(128)S(1)} all-reduce(f32[128]{0:T(128)S(1)} %get-tuple-element.14), channel_id=1, replica_groups=mesh['req'=16,'exp'=8] {'exp'}, use_global_device_ids=true, to_apply=%region_6.9 | all-reduce | flops 128 | bytes 1024 | tf_op jit(solution)/shard_map/psum | solution.py:116
  90.8 2.0 gather_fusion.3
  93.0 13.6 %all_to_all.54 = bf16[16,32,512]{2,1,0:T(8,128)(2,1)} all-to-all(bf16[16,32,512]{2,1,0:T(8,128)(2,1)S(1)} %select_select_fusion.3), channel_id=1, replica_groups=mesh['req'=16,'exp'=8] {'req'}, dimensions={0} | all-to-all | bytes 1048576 | tf_op jit(solution)/shard_map/all_to_all | solution.py:141
  106.6 28.7 %all-gather.5.cloned.1.call-done = bf16[512,4096]{1,0:T(8,128)(2,1)} async-done(((bf16[512,512]{1,0:T(8,128)(2,1)}), bf16[512,4096]{1,0:T(8,128)(2,1)}) %all-gather.5.cloned.1.call-update) | async-done | bytes 4194320 | tf_op jit(solution)/shard_map/all_gather | solution.py:142
  135.3 9.8 %fusion.4 = f32[512,896]{1,0:T(8,128)S(1)} fusion(bf16[512,4096]{1,0:T(8,128)(2,1)} %all-gather.5.cloned.1.call-done, bf16[1,4096,896]{2,1,0:T(8,128)(2,1)} %param.27), kind=kOutput, calls=%fused_computation.15 | convolution fusion | flops 3758096384 | bytes 13369344 | tf_op jit(solution)/shard_map/dot_general | solution.py:143
  145.1 16.3 %fusion.6 = bf16[512,4096]{1,0:T(8,128)(2,1)} fusion(bf16[1,896,4096]{2,1,0:T(8,128)(2,1)} %param.29, f32[512,896]{1,0:T(8,128)S(1)} %fusion.4, bf16[512,4096]{1,0:T(8,128)(2,1)} %all-gather.5.cloned.1.call-done, bf16[1,4096,896]{2,1,0:T(8,128)(2,1)} %param.28), kind=kOutput, calls=%fused_computation.17 | convolution fusion | flops 7521042432 | bytes 24903680 | tf_op jit(solution)/shard_map/dot_general | solution.py:147
  161.4 7.0 %all-to-all-start.3 = ((bf16[16,32,4096]{2,1,0:T(8,128)(2,1)}), bf16[16,32,4096]{2,1,0:T(8,128)(2,1)}, u32[]{:S(2)}, u32[]{:S(2)}) async-start(bf16[16,32,4096]{2,1,0:T(8,128)(2,1)} %bitcast.67), calls=%async_computation.3 | async-start | bytes 8388608 | tf_op jit(solution)/shard_map/all_to_all | solution.py:150
  169.3 13.8 %psum.15 = f32[128,8]{0,1:T(8,128)S(1)} all-reduce(f32[128,8]{0,1:T(8,128)S(1)} %fusion.25), channel_id=1, replica_groups=mesh['req'=16,'exp'=8] {'exp'}, use_global_device_ids=true, to_apply=%region_7.10 | all-reduce | flops 1024 | bytes 8192 | tf_op jit(solution)/shard_map/psum | solution.py:119
  183.1 49.0 %all-to-all-done.3 = bf16[16,32,4096]{2,1,0:T(8,128)(2,1)} async-done(((bf16[16,32,4096]{2,1,0:T(8,128)(2,1)}), bf16[16,32,4096]{2,1,0:T(8,128)(2,1)}, u32[]{:S(2)}, u32[]{:S(2)}) %all-to-all-start.3) | async-done | bytes 4194336 | tf_op jit(solution)/shard_map/all_to_all | solution.py:150
  232.1 6.6 %gather_fusion.4 = bf16[256,4096]{1,0:T(8,128)(2,1)S(1)} fusion(bf16[512,4096]{1,0:T(8,128)(2,1)} %bitcast.13, s32[1024]{0:T(1024)S(1)} %pad_clamp_fusion.1), kind=kCustom, calls=%fused_computation.8 | custom fusion | bytes 4195328 | tf_op jit(solution)/shard_map/jit(_take)/gather | solution.py:151
  238.8 2.7 gather.45
  241.4 4.0 %copy_select_fusion = bf16[128,2,4096]{2,0,1:T(8,128)(2,1)S(1)} fusion(bf16[128,2,4096]{2,1,0:T(2,128)(2,1)} %gather.45, pred[128,2]{0,1:T(4,128)(4,1)S(1)} %compare_and_fusion.3), kind=kLoop, calls=%fused_computation.22 | loop fusion | flops 1048576 | bytes 4194560 | tf_op jit(solution)/shard_map/jit(_take)/select_n | solution.py:151
  245.5 1.5 fusion.10
  247.2 15.8 %all_to_all.55 = bf16[16,4,4096]{2,1,0:T(4,128)(2,1)S(1)} all-to-all(bf16[16,4,4096]{2,1,0:T(4,128)(2,1)S(1)} %all_to_all.46), channel_id=1, replica_groups=mesh['req'=16,'exp'=8] {'req'}, dimensions={0} | all-to-all | bytes 1048576 | tf_op jit(solution)/shard_map/all_to_all | solution.py:87
  263.3 2.2 gather_fusion.9
  265.5 1.4 broadcast_select_fusion
  266.9 1.2 copy.134
  268.1 9.3 %reduce-scatter.2.cloned.1.call-done = bf16[128,512]{1,0:T(8,128)(2,1)} async-done(((bf16[128,4096]{1,0:T(8,128)(2,1)}), bf16[128,512]{1,0:T(8,128)(2,1)}) %reduce-scatter.2.cloned.1.call-update) | async-done | bytes 131088 | tf_op jit(solution)/shard_map/reduce_scatter | solution.py:155
  277.4 1.6 convert_add_fusion
  (115 shorter events, 17.9 us)
Async XLA Ops:
  7.2 32.1 %copy-start = (bf16[256,8,256]{2,1,0:T(8,128)(2,1)S(1)}, bf16[256,8,256]{2,1,0:T(8,128)(2,1)}, u32[]{:S(2)}) copy-start(bf16[256,8,256]{2,1,0:T(8,128)(2,1)} %param.22) | copy-start | bytes 3145732
  7.2 29.5 %copy-start.10 = (s32[128]{0:T(128)S(1)}, s32[128]{0:T(128)}, u32[]{:S(2)}) copy-start(s32[128]{0:T(128)} %param.24) | copy-start | bytes 1540
  7.2 66.2 %all-gather.3.cloned.1.call-start = ((), (), s32[]{:S(2)}) async-start(), calls=%async_computation.6 | async-start | bytes 4456448 | tf_op jit(solution)/shard_map/all_gather | solution.py:110
  23.1 26.5 %all-to-all-start = ((bf16[16,4,512]{2,1,0:T(4,128)(2,1)}), bf16[16,4,512]{2,1,0:T(4,128)(2,1)S(1)}, u32[]{:S(2)}, u32[]{:S(2)}) async-start(bf16[16,4,512]{2,1,0:T(4,128)(2,1)} %select_select_fusion.4), calls=%async_computation | async-start | bytes 131072 | tf_op jit(solution)/shard_map/all_to_all | solution.py:80
  39.2 4.1 %copy-start.4 = (bf16[128,4096]{1,0:T(8,128)(2,1)S(1)}, bf16[128,4096]{1,0:T(8,128)(2,1)}, u32[]{:S(2)}) copy-start(bf16[128,4096]{1,0:T(8,128)(2,1)} %param.17) | copy-start | bytes 3145732
  45.8 1.0 copy-start.2
  46.8 10.5 %copy-start.5 = (bf16[128,512]{1,0:T(8,128)(2,1)S(1)}, bf16[128,512]{1,0:T(8,128)(2,1)}, u32[]{:S(2)}) copy-start(bf16[128,512]{1,0:T(8,128)(2,1)} %param.18) | copy-start | bytes 393220
  49.6 22.2 %all-to-all-start.1 = ((bf16[16,4,4096]{2,1,0:T(4,128)(2,1)}), bf16[16,4,4096]{2,1,0:T(4,128)(2,1)S(1)}, u32[]{:S(2)}, u32[]{:S(2)}) async-start(bf16[16,4,4096]{2,1,0:T(4,128)(2,1)} %all_to_all.38), calls=%async_computation.1 | async-start | bytes 1048576 | tf_op jit(solution)/shard_map/all_to_all | solution.py:73
  56.9 78.5 %all-gather.5.cloned.1.call-start = ((), (), s32[]{:S(2)}) async-start(), calls=%async_computation.7 | async-start | bytes 4718592 | tf_op jit(solution)/shard_map/all_gather | solution.py:142
  73.4 17.4 %copy-start.9 = (f32[512]{0:T(512)S(1)}, f32[512]{0:T(512)}, u32[]{:S(2)}) copy-start(f32[512]{0:T(512)} %param.21) | copy-start | bytes 6148
  161.4 7.5 %copy-start.8 = (s32[128,2]{0,1:T(2,128)S(1)}, s32[128,2]{0,1:T(2,128)}, u32[]{:S(2)}) copy-start(s32[128,2]{0,1:T(2,128)} %param.26) | copy-start | bytes 3076
  161.4 7.5 %copy-start.7 = (f32[512,8]{0,1:T(8,128)S(1)}, f32[512,8]{0,1:T(8,128)}, u32[]{:S(2)}) copy-start(f32[512,8]{0,1:T(8,128)} %param.20) | copy-start | bytes 49156
  161.4 70.7 %all-to-all-start.3 = ((bf16[16,32,4096]{2,1,0:T(8,128)(2,1)}), bf16[16,32,4096]{2,1,0:T(8,128)(2,1)}, u32[]{:S(2)}, u32[]{:S(2)}) async-start(bf16[16,32,4096]{2,1,0:T(8,128)(2,1)} %bitcast.67), calls=%async_computation.3 | async-start | bytes 8388608 | tf_op jit(solution)/shard_map/all_to_all | solution.py:150
  168.4 109.0 %reduce-scatter.2.cloned.1.call-start = ((), (), s32[]{:S(2)}) async-start(), calls=%async_computation.8 | async-start | bytes 1179648 | tf_op jit(solution)/shard_map/reduce_scatter | solution.py:155
  245.4 1.5 copy-start.6
  246.9 16.2 %copy-start.3 = (bf16[128,4096]{1,0:T(8,128)(2,1)S(1)}, bf16[128,4096]{1,0:T(8,128)(2,1)}, u32[]{:S(2)}) copy-start(bf16[128,4096]{1,0:T(8,128)(2,1)} %copy-done.2) | copy-start | bytes 3145732
  263.3 15.8 %copy-start.1 = (bf16[256,8,256]{2,1,0:T(8,128)(2,1)S(1)}, bf16[256,8,256]{2,1,0:T(8,128)(2,1)}, u32[]{:S(2)}) copy-start(bf16[256,8,256]{2,1,0:T(8,128)(2,1)} %param.22) | copy-start | bytes 3145732
Sparse Core Ops, SparseCore 0:
  10.2 59.3 all-gather.2
  106.7 28.5 all-gather.4
  247.1 30.3 reduce-scatter.1
where the time goes:
time: 286 us
  waiting for transfers between devices  101 us (35%)
  blocking collectives  57.5 us (20%)
  local copies, waits for them, and re-layouts  40.8 us (14%)
  matrix products  29.5 us (10%)
  starting transfers between devices  21.5 us (8%)
  other arithmetic  20.6 us (7%)
  between operations  14.2 us (5%)
    all_to_all x1, waiting for transfers between devices, body(): lax.all_to_all(partial_value, 'req', split_axis=0, concat_axis=0, tiled=T...  49 us
    all_gather x1, waiting for transfers between devices, body(): rows_full = lax.all_gather(arrived, 'exp', axis=1, tiled=True)  28.7 us
    dot_general x1, matrix products, body(): jnp.dot(active, w_down[0], preferred_element_type=jnp.float32)  16.3 us
    all_to_all x1, blocking collectives, body(): lax.all_to_all(pick_rows(page_rows, send_index, send_live), 'req', split_...  15.8 us
    psum x1, blocking collectives, body(): total_sq = lax.psum(squares, 'exp')  14.3 us
    psum x1, blocking collectives, body(): lax.psum(jnp.dot(normed, router_w, precision=lax.Precision.HIGHEST), 'exp')  13.8 us
    all_to_all x1, waiting for transfers between devices, body(): lax.all_to_all(pick_rows(attention_out, send_index, send_live), 'req', sp...  13.6 us
    all_to_all x1, blocking collectives, body(): lax.all_to_all(outgoing, 'req', split_axis=0, concat_axis=0, tiled=True)  13.6 us
  transfers between devices with their start and end apart: 6, of which 4 were waited for; matrix products, arithmetic and copies ran while one was open for 15% of the time, Pallas kernels for 0%

commit v1 on v0

--- a/solution.py
+++ b/solution.py
@@ -139,7 +139,9 @@
     slot_live = jnp.any(chosen_slot, axis=2).reshape(-1)
     outgoing = pick_rows(normed_rows, slot_source, slot_live)
     arrived = lax.all_to_all(outgoing, "req", split_axis=0, concat_axis=0, tiled=True)
-    rows_full = lax.all_gather(arrived, "exp", axis=1, tiled=True)
+    rows_full = jnp.concatenate(
+        lax.all_to_all(jnp.stack([arrived] * lax.axis_size("exp")), "exp", 0, 0), axis=1
+    )
     gate_h = jnp.dot(rows_full, w_gate[0], preferred_element_type=jnp.float32)
     up_h = jnp.dot(rows_full, w_up[0], preferred_element_type=jnp.float32)
     active = (jax.nn.silu(gate_h) * up_h).astype(jnp.bfloat16)

time: 286 us -> 307 us (1.073)
  blocking collectives: 57.5 us -> 109 us
  waiting for transfers between devices: 101 us -> 72.4 us
    all_to_all x0 -> x1, blocking collectives: none -> 53.2 us  [body(): lax.all_to_all(jnp.stack([arrived] * lax.axis_size('exp')), 'exp', 0, 0)]
    all_gather x1 -> x0, waiting for transfers between devices: 28.7 us -> none  [body(): rows_full = lax.all_gather(arrived, 'exp', axis=1, tiled=True)]
    unnamed x27 -> x29, local copies, waits for them, and re-layouts: 4.33 us -> 6.3 us
  transfers between devices with their start and end apart: 6 -> 5, of which waited for: 4 -> 3; matrix products, arithmetic and copies ran while one was open for 15% -> 14% of each run, Pallas kernels for 0% -> 0%
where the time goes in v1:
time: 307 us; the launch traced here: 306 us
  blocking collectives  109 us (36%)
  waiting for transfers between devices  72.4 us (24%)
  local copies, waits for them, and re-layouts  43.4 us (14%)
  matrix products  27 us (9%)
  other arithmetic  20.6 us (7%)
  starting transfers between devices  19.1 us (6%)
  between operations  14.5 us (5%)
    all_to_all x1, blocking collectives, body(): lax.all_to_all(jnp.stack([arrived] * lax.axis_size('exp')), 'exp', 0, 0)  53.2 us
    all_to_all x1, waiting for transfers between devices, body(): lax.all_to_all(partial_value, 'req', split_axis=0, concat_axis=0, tiled=T...  48.4 us
    dot_general x1, matrix products, body(): jnp.dot(active, w_down[0], preferred_element_type=jnp.float32)  16.4 us
    all_to_all x1, blocking collectives, body(): lax.all_to_all(pick_rows(page_rows, send_index, send_live), 'req', split_...  14.8 us
    psum x1, blocking collectives, body(): total_sq = lax.psum(squares, 'exp')  14.3 us
    all_to_all x1, waiting for transfers between devices, body(): lax.all_to_all(pick_rows(attention_out, send_index, send_live), 'req', sp...  13.7 us
    psum x1, blocking collectives, body(): lax.psum(jnp.dot(normed, router_w, precision=lax.Precision.HIGHEST), 'exp')  13.6 us
    all_to_all x1, blocking collectives, body(): lax.all_to_all(outgoing, 'req', split_axis=0, concat_axis=0, tiled=True)  12.9 us
  transfers between devices with their start and end apart: 5, of which 3 were waited for; matrix products, arithmetic and copies ran while one was open for 14% of the time, Pallas kernels for 0%

profile of v1, /device:TPU:0, one launch (start us, length us, event | category | flops | bytes accessed | tf_op | source)
XLA Modules:
  0.0 305.9 jit_solution(6368292855565957230)
XLA Ops:
  8.6 8.0 %scatter_custom_fusion = s32[2048]{0:T(1024)S(1)} fusion(s32[2048]{0:T(1024)S(1)} %compare_select_fusion.1, s32[2048]{0:T(1024)S(1)} %iota.72, s32[]{:T(128)} %constant.182.clone.1), kind=kCustom, calls=%fused_computation.93 | custom fusion | bytes 8196 | tf_op jit(solution)/shard_map/scatter | solution.py:43
  16.9 2.8 select_reduce_fusion
  20.7 1.6 gather_fusion.1
  23.1 7.1 %all-to-all-start = ((bf16[16,4,512]{2,1,0:T(4,128)(2,1)}), bf16[16,4,512]{2,1,0:T(4,128)(2,1)S(1)}, u32[]{:S(2)}, u32[]{:S(2)}) async-start(bf16[16,4,512]{2,1,0:T(4,128)(2,1)} %select_select_fusion.4), calls=%async_computation | async-start | bytes 131072 | tf_op jit(solution)/shard_map/all_to_all | solution.py:80
  35.3 1.1 gather_fusion
  39.2 1.7 gather_fusion.5
  41.0 2.4 gather.47
  44.2 1.6 select_select_fusion
  49.6 7.2 %all-to-all-start.1 = ((bf16[16,4,4096]{2,1,0:T(4,128)(2,1)}), bf16[16,4,4096]{2,1,0:T(4,128)(2,1)S(1)}, u32[]{:S(2)}, u32[]{:S(2)}) async-start(bf16[16,4,4096]{2,1,0:T(4,128)(2,1)} %all_to_all.39), calls=%async_computation.1 | async-start | bytes 1048576 | tf_op jit(solution)/shard_map/all_to_all | solution.py:73
  58.2 13.7 %all-to-all-done.1 = bf16[16,4,4096]{2,1,0:T(4,128)(2,1)S(1)} async-done(((bf16[16,4,4096]{2,1,0:T(4,128)(2,1)}), bf16[16,4,4096]{2,1,0:T(4,128)(2,1)S(1)}, u32[]{:S(2)}, u32[]{:S(2)}) %all-to-all-start.1) | async-done | bytes 524320 | tf_op jit(solution)/shard_map/all_to_all | solution.py:73
  72.2 1.2 gather_fusion.7
  73.4 3.0 multiply_reduce_fusion
  76.4 14.3 %psum.14 = f32[128]{0:T(128)S(1)} all-reduce(f32[128]{0:T(128)S(1)} %get-tuple-element.14), channel_id=1, replica_groups=mesh['req'=16,'exp'=8] {'exp'}, use_global_device_ids=true, to_apply=%region_6.9 | all-reduce | flops 128 | bytes 1024 | tf_op jit(solution)/shard_map/psum | solution.py:116
  90.8 2.0 gather_fusion.3
  93.0 12.9 %all_to_all.56 = bf16[16,32,512]{2,1,0:T(8,128)(2,1)S(1)} all-to-all(bf16[16,32,512]{2,1,0:T(8,128)(2,1)S(1)} %select_select_fusion.3), channel_id=1, replica_groups=mesh['req'=16,'exp'=8] {'req'}, dimensions={0} | all-to-all | bytes 1048576 | tf_op jit(solution)/shard_map/all_to_all | solution.py:141
  106.5 53.2 %all_to_all.57 = bf16[8,512,512]{1,2,0:T(8,128)(2,1)S(1)} all-to-all(bf16[8,512,512]{1,2,0:T(8,128)(2,1)S(1)} %stack.5), channel_id=1, replica_groups=mesh['req'=16,'exp'=8] {'exp'}, dimensions={0} | all-to-all | bytes 8388608 | tf_op jit(solution)/shard_map/all_to_all | solution.py:143
  159.7 2.0 copy-done.5
  161.7 7.2 %fusion.4 = f32[512,896]{1,0:T(8,128)S(1)} fusion(bf16[512,4096]{0,1:T(8,128)(2,1)S(1)} %bitcast.71, bf16[1,4096,896]{2,1,0:T(8,128)(2,1)} %param.27), kind=kOutput, calls=%fused_computation.15 | convolution fusion | flops 3758096384 | bytes 13369344 | tf_op jit(solution)/shard_map/dot_general | solution.py:145
  168.9 16.4 %fusion.6 = bf16[512,4096]{1,0:T(8,128)(2,1)} fusion(bf16[1,896,4096]{2,1,0:T(8,128)(2,1)} %param.29, f32[512,896]{1,0:T(8,128)S(1)} %fusion.4, bf16[512,4096]{0,1:T(8,128)(2,1)} %bitcast.72, bf16[1,4096,896]{2,1,0:T(8,128)(2,1)} %param.28), kind=kOutput, calls=%fused_computation.17 | convolution fusion | flops 7521042432 | bytes 24903680 | tf_op jit(solution)/shard_map/dot_general | solution.py:149
  185.3 4.7 %all-to-all-start.4 = ((bf16[16,32,4096]{2,1,0:T(8,128)(2,1)}), bf16[16,32,4096]{2,1,0:T(8,128)(2,1)}, u32[]{:S(2)}, u32[]{:S(2)}) async-start(bf16[16,32,4096]{2,1,0:T(8,128)(2,1)} %bitcast.70), calls=%async_computation.4 | async-start | bytes 8388608 | tf_op jit(solution)/shard_map/all_to_all | solution.py:152
  190.8 13.6 %psum.15 = f32[128,8]{0,1:T(8,128)S(1)} all-reduce(f32[128,8]{0,1:T(8,128)S(1)} %fusion.26), channel_id=1, replica_groups=mesh['req'=16,'exp'=8] {'exp'}, use_global_device_ids=true, to_apply=%region_7.10 | all-reduce | flops 1024 | bytes 8192 | tf_op jit(solution)/shard_map/psum | solution.py:119
  204.5 48.4 %all-to-all-done.4 = bf16[16,32,4096]{2,1,0:T(8,128)(2,1)} async-done(((bf16[16,32,4096]{2,1,0:T(8,128)(2,1)}), bf16[16,32,4096]{2,1,0:T(8,128)(2,1)}, u32[]{:S(2)}, u32[]{:S(2)}) %all-to-all-start.4) | async-done | bytes 4194336 | tf_op jit(solution)/shard_map/all_to_all | solution.py:152
  252.9 6.6 %gather_fusion.4 = bf16[256,4096]{1,0:T(8,128)(2,1)S(1)} fusion(bf16[512,4096]{1,0:T(8,128)(2,1)} %bitcast.16, s32[1024]{0:T(1024)S(1)} %pad_clamp_fusion.1), kind=kCustom, calls=%fused_computation.8 | custom fusion | bytes 4195328 | tf_op jit(solution)/shard_map/jit(_take)/gather | solution.py:153
  259.5 2.7 gather.45
  262.1 4.0 %copy_select_fusion = bf16[128,2,4096]{2,0,1:T(8,128)(2,1)S(1)} fusion(bf16[128,2,4096]{2,1,0:T(2,128)(2,1)} %gather.45, pred[128,2]{0,1:T(4,128)(4,1)S(1)} %compare_and_fusion.3), kind=kLoop, calls=%fused_computation.22 | loop fusion | flops 1048576 | bytes 4194560 | tf_op jit(solution)/shard_map/jit(_take)/select_n | solution.py:153
  266.2 1.5 fusion.10
  267.9 14.8 %all_to_all.58 = bf16[16,4,4096]{2,1,0:T(4,128)(2,1)S(1)} all-to-all(bf16[16,4,4096]{2,1,0:T(4,128)(2,1)S(1)} %all_to_all.47), channel_id=1, replica_groups=mesh['req'=16,'exp'=8] {'req'}, dimensions={0} | all-to-all | bytes 1048576 | tf_op jit(solution)/shard_map/all_to_all | solution.py:87
  283.0 2.2 gather_fusion.9
  285.2 1.4 broadcast_select_fusion
  286.6 1.2 copy.139
  287.8 9.6 %reduce-scatter.2.cloned.1.call-done = bf16[128,512]{1,0:T(8,128)(2,1)} async-done(((bf16[128,4096]{1,0:T(8,128)(2,1)}), bf16[128,512]{1,0:T(8,128)(2,1)}) %reduce-scatter.2.cloned.1.call-update) | async-done | bytes 131088 | tf_op jit(solution)/shard_map/reduce_scatter | solution.py:157
  297.4 1.6 convert_add_fusion
  (117 shorter events, 19.5 us)
Async XLA Ops:
  7.2 32.1 %copy-start = (bf16[256,8,256]{2,1,0:T(8,128)(2,1)S(1)}, bf16[256,8,256]{2,1,0:T(8,128)(2,1)}, u32[]{:S(2)}) copy-start(bf16[256,8,256]{2,1,0:T(8,128)(2,1)} %param.22) | copy-start | bytes 3145732
  7.2 29.5 %copy-start.11 = (s32[128]{0:T(128)S(1)}, s32[128]{0:T(128)}, u32[]{:S(2)}) copy-start(s32[128]{0:T(128)} %param.24) | copy-start | bytes 1540
  7.2 66.2 %all-gather.2.cloned.1.call-start = ((), (), s32[]{:S(2)}) async-start(), calls=%async_computation.7 | async-start | bytes 4456448 | tf_op jit(solution)/shard_map/all_gather | solution.py:110
  23.1 26.5 %all-to-all-start = ((bf16[16,4,512]{2,1,0:T(4,128)(2,1)}), bf16[16,4,512]{2,1,0:T(4,128)(2,1)S(1)}, u32[]{:S(2)}, u32[]{:S(2)}) async-start(bf16[16,4,512]{2,1,0:T(4,128)(2,1)} %select_select_fusion.4), calls=%async_computation | async-start | bytes 131072 | tf_op jit(solution)/shard_map/all_to_all | solution.py:80
  39.2 4.1 %copy-start.4 = (bf16[128,4096]{1,0:T(8,128)(2,1)S(1)}, bf16[128,4096]{1,0:T(8,128)(2,1)}, u32[]{:S(2)}) copy-start(bf16[128,4096]{1,0:T(8,128)(2,1)} %param.17) | copy-start | bytes 3145732
  45.8 1.0 copy-start.2
  46.8 10.5 %copy-start.6 = (bf16[128,512]{1,0:T(8,128)(2,1)S(1)}, bf16[128,512]{1,0:T(8,128)(2,1)}, u32[]{:S(2)}) copy-start(bf16[128,512]{1,0:T(8,128)(2,1)} %param.18) | copy-start | bytes 393220
  49.6 22.2 %all-to-all-start.1 = ((bf16[16,4,4096]{2,1,0:T(4,128)(2,1)}), bf16[16,4,4096]{2,1,0:T(4,128)(2,1)S(1)}, u32[]{:S(2)}, u32[]{:S(2)}) async-start(bf16[16,4,4096]{2,1,0:T(4,128)(2,1)} %all_to_all.39), calls=%async_computation.1 | async-start | bytes 1048576 | tf_op jit(solution)/shard_map/all_to_all | solution.py:73
  73.4 17.4 %copy-start.10 = (f32[512]{0:T(512)S(1)}, f32[512]{0:T(512)}, u32[]{:S(2)}) copy-start(f32[512]{0:T(512)} %param.21) | copy-start | bytes 6148
  159.7 2.0 copy-start.5
  185.3 5.1 %copy-start.9 = (s32[128,2]{0,1:T(2,128)S(1)}, s32[128,2]{0,1:T(2,128)}, u32[]{:S(2)}) copy-start(s32[128,2]{0,1:T(2,128)} %param.26) | copy-start | bytes 3076
  185.3 5.2 %copy-start.8 = (f32[512,8]{0,1:T(8,128)S(1)}, f32[512,8]{0,1:T(8,128)}, u32[]{:S(2)}) copy-start(f32[512,8]{0,1:T(8,128)} %param.20) | copy-start | bytes 49156
  185.3 67.6 %all-to-all-start.4 = ((bf16[16,32,4096]{2,1,0:T(8,128)(2,1)}), bf16[16,32,4096]{2,1,0:T(8,128)(2,1)}, u32[]{:S(2)}, u32[]{:S(2)}) async-start(bf16[16,32,4096]{2,1,0:T(8,128)(2,1)} %bitcast.70), calls=%async_computation.4 | async-start | bytes 8388608 | tf_op jit(solution)/shard_map/all_to_all | solution.py:152
  189.9 107.5 %reduce-scatter.2.cloned.1.call-start = ((), (), s32[]{:S(2)}) async-start(), calls=%async_computation.8 | async-start | bytes 1179648 | tf_op jit(solution)/shard_map/reduce_scatter | solution.py:157
  266.2 1.5 copy-start.7
  267.6 15.2 %copy-start.3 = (bf16[128,4096]{1,0:T(8,128)(2,1)S(1)}, bf16[128,4096]{1,0:T(8,128)(2,1)}, u32[]{:S(2)}) copy-start(bf16[128,4096]{1,0:T(8,128)(2,1)} %copy-done.2) | copy-start | bytes 3145732
  283.0 16.1 %copy-start.1 = (bf16[256,8,256]{2,1,0:T(8,128)(2,1)S(1)}, bf16[256,8,256]{2,1,0:T(8,128)(2,1)}, u32[]{:S(2)}) copy-start(bf16[256,8,256]{2,1,0:T(8,128)(2,1)} %param.22) | copy-start | bytes 3145732
Sparse Core Ops, SparseCore 0:
  10.2 59.3 all-gather.1
  267.8 29.5 reduce-scatter.1
